TPU v7x, 256 devices: a whole 4x4x8 slice. The times are simulated.
256 devices in a mesh: depth: 32 (over y, x, core), rows: 8 (over z).
Axes of the slice: x: 4, y: 4, z: 8, core: 2. Of those that a mesh axis runs over, the one named last changes fastest.
Arguments:
- initial: float32 [32, 256, 128], P('rows'), may hold values from -6 to 6
- forward_guess: float32 [64, 32, 256, 128], P('depth', 'rows'), may hold values from -6 to 6
- adjoint_guess: float32 [64, 32, 256, 128], P('depth', 'rows'), may hold values from -6 to 6
- cotangent: float32 [32, 256, 128], P('rows'), may hold values from -6 to 6
- kernel: bfloat16 [3, 3, 128, 128], replicated, may hold values from -0.125 to 0.125
- conv_bias: float32 [128], replicated, may hold values from -1.5 to 1.5
Outputs:
- states: float32 [64, 32, 256, 128], P('depth', 'rows')
- adjoints: float32 [64, 32, 256, 128], P('depth', 'rows')
- grad_kernel: float32 [3, 3, 128, 128], replicated
- grad_bias: float32 [128], replicated
All inputs are finite; a program needn't handle non-finite values.
Results may differ from a plain program's by a relative error of at most 0.0025.
The roundings to bfloat16 on the way count: a program that leaves them out, or rounds other values in their place, can miss the bound.
Values may be sent and summed in bfloat16 or wider, within the bound.
No kernel may reach another device: no remote copies, remote signals or barrier semaphores. Data moves between devices by JAX's collectives and lax.ppermute only.
A program may use at most 64 MiB of HBM per device.

v0:
```python
import jax
import jax.numpy as jnp
from jax import lax
from jax.sharding import PartitionSpec as P

STEP_SIZE = 0.2


def padded_2(shard, sides, width):
    for axis, dim in sides:
        devices, length = (lax.axis_size(axis), shard.shape[dim])
        up = [(i, (i + 1) % devices) for i in range(devices - 1)]
        down = [(j, i) for i, j in up]
        last = lax.slice_in_dim(shard, length - width, length, axis=dim)
        leading = lax.slice_in_dim(shard, 0, width, axis=dim)
        before = lax.ppermute(last, axis, up)
        after = lax.ppermute(leading, axis, down)
        shard = jnp.concatenate([before, shard, after], axis=dim)
    return shard


def passed_along(value, axis, steps):
    count = lax.axis_size(axis)
    leading, last = (max(0, -steps), min(count, count - steps))
    return lax.ppermute(value, axis, [(source, source + steps) for source in range(leading, last)])


def restrict(signal):
    row_count, col_count, channels = signal.shape
    return signal.reshape(row_count // 2, 2, col_count // 2, 2, channels).mean(axis=(1, 3))


def prolong(signal):
    return jnp.repeat(jnp.repeat(signal, 2, axis=0), 2, axis=1)


def taps_product(padded, kernel, row_count, col_count):
    summed = jnp.zeros((row_count * col_count, kernel.shape[3]), jnp.float32)
    for row_tap in range(3):
        for col_tap in range(3):
            window = padded[row_tap : row_tap + row_count, col_tap : col_tap + col_count].reshape(
                row_count * col_count, -1
            )
            summed = summed + jnp.dot(
                window, kernel[row_tap, col_tap], preferred_element_type=jnp.float32
            )
    return summed.reshape(row_count, col_count, -1)


def surround(signal, on_coarse):
    if on_coarse:
        padded = padded_2(signal, (("rows", 0),), 1)
    else:
        padded = padded_2(signal, (("rows", 0),), 1)
    return jnp.pad(padded, ((0, 0), (1, 1), (0, 0)))


def advance(current, kernel, conv_bias, on_coarse):
    factor = 2.0 * STEP_SIZE if on_coarse else STEP_SIZE
    squashed = jnp.tanh(current).astype(jnp.bfloat16)
    padded = surround(squashed, on_coarse)
    return current + factor * (
        taps_product(padded, kernel, current.shape[0], current.shape[1]) + conv_bias
    )


def retreat(current, adjoint, kernel_flip, on_coarse):
    factor = 2.0 * STEP_SIZE if on_coarse else STEP_SIZE
    derivative = 1.0 - jnp.tanh(current) ** 2
    padded = surround(adjoint.astype(jnp.bfloat16), on_coarse)
    return adjoint + factor * derivative * taps_product(
        padded, kernel_flip, adjoint.shape[0], adjoint.shape[1]
    )


def kernel_terms(padded, cotan, row_count, col_count):
    flat = cotan.reshape(row_count * col_count, -1)
    tap_rows = []
    for row_tap in range(3):
        tap_cols = []
        for col_tap in range(3):
            window = padded[row_tap : row_tap + row_count, col_tap : col_tap + col_count].reshape(
                row_count * col_count, -1
            )
            tap_cols.append(
                lax.dot_general(
                    window, flat, (((0,), (0,)), ((), ())), preferred_element_type=jnp.float32
                )
            )
        tap_rows.append(jnp.stack(tap_cols))
    return jnp.stack(tap_rows)


def shards(initial, forward_guess, adjoint_guess, cotangent, kernel, conv_bias):
    block_count = lax.axis_size("depth")
    depth_pos = lax.axis_index("depth")
    at_first = depth_pos == 0
    at_last = depth_pos == block_count - 1
    row_count, col_count = (initial.shape[0], initial.shape[1])
    kernel_flip = jnp.transpose(jnp.flip(kernel, (0, 1)), (0, 1, 3, 2))
    coarse_start = restrict(initial)
    guess_point = forward_guess[1]
    previous = passed_along(guess_point, "depth", 1)
    previous = jnp.where(at_first, initial, previous)
    relaxed_odd = advance(previous, kernel, conv_bias, False)
    rhs_local = restrict(advance(relaxed_odd, kernel, conv_bias, False)) - advance(
        restrict(previous), kernel, conv_bias, True
    )

    def forward_turn(step_no, state_pair):
        incoming, kept_state = state_pair
        result = advance(incoming, kernel, conv_bias, True) + rhs_local
        kept_state = jnp.where(step_no == depth_pos, result, kept_state)
        incoming = passed_along(result, "depth", 1)
        return (incoming, kept_state)

    last_coarse, stored = lax.fori_loop(
        0, block_count, forward_turn, (coarse_start, jnp.zeros_like(coarse_start))
    )
    corrected = guess_point + prolong(stored - restrict(guess_point))
    prev_fixed, prev_coarse = passed_along((corrected, stored), "depth", 1)
    prev_fixed = jnp.where(at_first, initial, prev_fixed)
    linear = jnp.where(at_first, coarse_start, prev_coarse)
    state_odd = advance(prev_fixed, kernel, conv_bias, False)
    guess_even = adjoint_guess[0]
    ahead = passed_along(guess_even, "depth", -1)
    ahead = jnp.where(at_last, cotangent, ahead)
    relaxed_adj = retreat(state_odd, ahead, kernel_flip, False)
    residual = retreat(prev_fixed, relaxed_adj, kernel_flip, False) - guess_even
    coarse_res = restrict(residual)

    def backward_turn(step_no, state_pair):
        incoming, kept_error = state_pair
        result = retreat(linear, incoming, kernel_flip, True) + coarse_res
        kept_error = jnp.where(step_no == block_count - 1 - depth_pos, result, kept_error)
        incoming = passed_along(result, "depth", -1)
        return (incoming, kept_error)

    final_error, error_own = lax.fori_loop(
        0, block_count, backward_turn, (jnp.zeros_like(coarse_start), jnp.zeros_like(coarse_start))
    )
    corrected_adj = guess_even + prolong(error_own)
    ahead_fixed = passed_along(corrected_adj, "depth", -1)
    ahead_fixed = jnp.where(at_last, cotangent, ahead_fixed)
    adjoint_odd = retreat(state_odd, ahead_fixed, kernel_flip, False)
    squashed_even = surround(jnp.tanh(prev_fixed).astype(jnp.bfloat16), False)
    squashed_odd = surround(jnp.tanh(state_odd).astype(jnp.bfloat16), False)
    local_grad = kernel_terms(squashed_even, adjoint_odd.astype(jnp.bfloat16), row_count, col_count)
    local_grad = local_grad + kernel_terms(
        squashed_odd, ahead_fixed.astype(jnp.bfloat16), row_count, col_count
    )
    local_bias = jnp.sum(adjoint_odd, axis=(0, 1)) + jnp.sum(ahead_fixed, axis=(0, 1))
    grad_sum, bias_sum = lax.psum((local_grad, local_bias), ("depth", "rows"))
    factor = STEP_SIZE / (row_count * lax.axis_size("rows") * col_count)
    states_out = jnp.stack([state_odd, corrected])
    adjoints_out = jnp.stack([corrected_adj, adjoint_odd])
    return (states_out, adjoints_out, grad_sum * factor, bias_sum * factor)


def solution(mesh):
    placed = (
        P("rows", None, None),
        P("depth", "rows", None, None),
        P("depth", "rows", None, None),
        P("rows", None, None),
        P(),
        P(),
    )
    return jax.shard_map(
        shards,
        mesh=mesh,
        in_specs=placed,
        out_specs=(P("depth", "rows", None, None), P("depth", "rows", None, None), P(), P()),
        check_vma=False,
    )
```

profile of v0, /device:TPU:1, one launch (start us, length us, event | category | flops | bytes accessed | tf_op | source)
XLA Modules:
  0.0 1818.0 jit_solution(15526250043578704130)
XLA Ops:
  127.0 579.7 %while.36 = (s32[]{:T(128)}, f32[2,128,128]{2,1,0:T(8,128)S(1)}, f32[2,128,128]{2,1,0:T(8,128)S(1)}, bf16[3,3,128,128]{3,2,1,0:T(8,128)(2,1)S(1)}, f32[128]{0:T(...) while((s32[]{:T(128)}, f32[2,128,128]{2,1,0:T(8,128)S(1)}, ...), condition=%wide.region_4.5_spmd.clone, body=%wide.region_3.4_spmd.clone.sunk | while | flops 76853248 | bytes 6327017 | solution.py:117
  355.8 7.6 collective-permute-start.2
  374.8 7.6 collective-permute-start.2
  393.7 7.6 collective-permute-start.2
  412.7 7.6 collective-permute-start.2
  431.7 7.6 collective-permute-start.2
  450.6 7.6 collective-permute-start.2
  469.6 7.6 collective-permute-start.2
  488.5 7.6 collective-permute-start.2
  507.5 7.6 collective-permute-start.2
  526.5 7.6 collective-permute-start.2
  545.4 7.6 collective-permute-start.2
  564.4 7.6 collective-permute-start.2
  583.4 7.6 collective-permute-start.2
  602.3 7.6 collective-permute-start.2
  621.3 7.6 collective-permute-start.2
  640.3 7.6 collective-permute-start.2
  678.2 7.6 collective-permute-start.2
  810.8 659.7 %while.37 = (s32[]{:T(128)}, f32[2,128,128]{2,1,0:T(8,128)S(1)}, f32[2,128,128]{2,1,0:T(8,128)S(1)}, f32[2,128,128]{2,1,0:T(8,128)S(1)}, bf16[3,3,128,128]{3,2,1...) while((s32[]{:T(128)}, f32[2,128,128]{2,1,0:T(8,128)S(1)}, ...), condition=%wide.region_8.9_spmd.clone, body=%wide.region_7.8_spmd.clone.sunk | while | flops 76886016 | bytes 7244093 | solution.py:139
  824.9 10.2 collective-permute-done.5
  868.0 10.2 collective-permute-done.5
  911.1 10.8 collective-permute-done.5
  1531.3 105.2 %psum.15 = f32[128]{0:T(128)S(1)} all-reduce(f32[128]{0:T(128)S(1)} %add.599), channel_id=1, replica_groups=mesh['depth'=32,'rows'=8] {'depth','rows'}, use_global_device_ids=true, to_apply=%region_12.13 | all-reduce | flops 128 | bytes 1024 | tf_op jit(solution)/shard_map/psum | solution.py:153
  1637.0 172.2 %all-reduce.12.cloned.1.call-done = f32[3,3,128,128]{3,2,1,0:T(8,128)} async-done(((f32[3,3,128,128]{3,2,1,0:T(8,128)}), f32[3,3,128,128]{3,2,1,0:T(8,128)}) %all-reduce.12.cloned.1.call-update) | async-done | bytes 589840 | tf_op jit(solution)/shard_map/psum | solution.py:153
  (1960 shorter events, 1355.9 us)
Async XLA Ops:
  7.2 1802.1 %all-reduce.12.cloned.1.call-start = ((), (), s32[]{:S(2)}) async-start(), calls=%async_computation | async-start | bytes 1179648 | tf_op jit(solution)/shard_map/psum | solution.py:153
  8.4 13.3 collective-permute-start.17
  27.8 16.5 collective-permute-start.11
  31.3 14.3 collective-permute-start.12
  35.0 14.3 collective-permute-start.18
  39.0 10.3 collective-permute-start.19
  40.3 19.8 %collective-permute-start.7 = (bf16[1,256,128]{1,2,0:T(8,128)(2,1)}, bf16[1,256,128]{1,2,0:T(8,128)(2,1)S(1)}, u32[]{:S(2)}, u32[]{:S(2)}) collective-permute-start(bf16[1,256,128]{1,2,0:T(8,128)(2,1)} %get-tuple-element.543), channel_id=1, source_target_pairs={{0,1},{1,2},{2,3},{3,4},{4,5},{5,6},{6,7},{8,9},{9,10},{10,11},{11... | collective-permute-start | bytes 196616 | tf_op jit(solution)/shard_map/ppermute | solution.py:16
  44.3 15.8 collective-permute-start.8
  85.2 13.3 collective-permute-start.10
  86.5 12.0 collective-permute-start.9
  355.8 9.5 collective-permute-start.2
  393.7 9.5 collective-permute-start.2
  412.7 9.5 collective-permute-start.2
  708.0 13.0 collective-permute-start.13
  723.7 16.0 collective-permute-start.14
  728.8 10.8 collective-permute-start.15
  731.3 42.4 %collective-permute-start.16 = (f32[2,128,128]{2,1,0:T(8,128)S(1)}, f32[2,128,128]{2,1,0:T(8,128)}, u32[]{:S(2)}, u32[]{:S(2)}) collective-permute-start(f32[2,128,128]{2,1,0:T(8,128)S(1)} %get-tuple-element.361), channel_id=1, source_target_pairs={{0,8},{8,16},{16,24},{24,32},{32,40},{40,48},{48,56},{56,64},{64,7... | collective-permute-start | bytes 393224 | tf_op jit(solution)/shard_map/ppermute | solution.py:25
  765.8 9.7 collective-permute-start.20
  823.0 12.2 collective-permute-start.5
  866.0 12.1 collective-permute-start.5
  909.1 12.7 collective-permute-start.5
  1475.5 18.2 %collective-permute-start.22 = (f32[4,256,128]{1,2,0:T(8,128)}, f32[4,256,128]{1,2,0:T(8,128)}, u32[]{:S(2)}, u32[]{:S(2)}) collective-permute-start(f32[4,256,128]{1,2,0:T(8,128)} %bitcast_add_fusion), channel_id=1, source_target_pairs={{8,0},{16,8},{24,16},{32,24},{40,32},{48,40},{56,48},{64,56},{72,6... | collective-permute-start | bytes 1572872 | tf_op jit(solution)/shard_map/ppermute | solution.py:25
  1480.7 12.7 collective-permute-start.25
  1498.4 9.9 collective-permute-start.23
  (370 other events, 2269.7 us)
Sparse Core Ops, SparseCore 0:
  1529.7 279.5 all-reduce.11
where the time goes:
time: 1830 us; the launch traced here: 1820 us
  starting transfers between devices  785 us (43%)
  waiting for transfers between devices  524 us (29%)
  local copies, waits for them, and re-layouts  184 us (10%)
  matrix products  117 us (6%)
  blocking collectives  105 us (6%)
  other arithmetic  78.5 us (4%)
    ppermute x72, starting transfers between devices, padded_2(): before = lax.ppermute(last, axis, up)  393 us
    ppermute x69, starting transfers between devices, passed_along(): lax.ppermute(value, axis, [(source, source + steps) for source in range(l...  299 us
    ppermute x69, waiting for transfers between devices, passed_along(): lax.ppermute(value, axis, [(source, source + steps) for source in range(l...  283 us
    psum x1, waiting for transfers between devices, shards(): grad_sum, bias_sum = lax.psum((local_grad, local_bias), ('depth', 'rows'))  172 us
    dot_general x639, matrix products, taps_product(): jnp.dot(window, kernel[row_tap, col_tap], preferred_element_type=jnp.floa...  113 us
    psum x1, blocking collectives, shards(): grad_sum, bias_sum = lax.psum((local_grad, local_bias), ('depth', 'rows'))  105 us
    ppermute x72, starting transfers between devices, padded_2(): after = lax.ppermute(leading, axis, down)  93.1 us
    slice x119, local copies, waits for them, and re-layouts, taps_product(): padded[row_tap:row_tap + row_count, col_tap:col_tap + col_count]  79.3 us
  transfers between devices with their start and end apart: 214, of which 132 were waited for; matrix products, arithmetic and copies ran while one was open for 4% of the time, Pallas kernels for 0%

commit v1 on v0

--- a/solution.py
+++ b/solution.py
@@ -4,6 +4,14 @@
 from jax.sharding import PartitionSpec as P
 
 STEP_SIZE = 0.2
+
+
+def compute_the_side(w_in):
+    link_axis = "rows"
+    along_axis = "depth"
+    for tick in (along_axis, link_axis):
+        w_in = lax.psum(w_in, tick)
+    return w_in
 
 
 def padded_2(shard, sides, width):
@@ -150,7 +158,7 @@
         squashed_odd, ahead_fixed.astype(jnp.bfloat16), row_count, col_count
     )
     local_bias = jnp.sum(adjoint_odd, axis=(0, 1)) + jnp.sum(ahead_fixed, axis=(0, 1))
-    grad_sum, bias_sum = lax.psum((local_grad, local_bias), ("depth", "rows"))
+    grad_sum, bias_sum = compute_the_side((local_grad, local_bias))
     factor = STEP_SIZE / (row_count * lax.axis_size("rows") * col_count)
     states_out = jnp.stack([state_odd, corrected])
     adjoints_out = jnp.stack([corrected_adj, adjoint_odd])

time: 1830 us -> 1690 us (0.923)
  local copies, waits for them, and re-layouts: 184 us -> 125 us
  waiting for transfers between devices: 524 us -> 490 us
  blocking collectives: 105 us -> 76.5 us
  other arithmetic: 78.5 us -> 55.6 us
    while x192 -> x0, local copies, waits for them, and re-layouts: 36.7 us -> none
    psum x1 -> x2, waiting for transfers between devices: 172 us -> 136 us  [compute_the_side(): w_in = lax.psum(w_in, tick)]
    psum x1 -> x2, blocking collectives: 105 us -> 76.5 us  [compute_the_side(): w_in = lax.psum(w_in, tick)]
    select_n x32, other arithmetic: 23.5 us -> 3.13 us  [backward_turn(): jnp.where(step_no == block_count - 1 - depth_pos, result, kept_error)]
    slice x72, local copies, waits for them, and re-layouts: 24.1 us -> 4.45 us  [padded_2(): last = lax.slice_in_dim(shard, length - width, length, axis=dim)]
  transfers between devices with their start and end apart: 214 -> 215, of which waited for: 132 -> 133; matrix products, arithmetic and copies ran while one was open for 4% -> 4% of each run, Pallas kernels for 0% -> 0%
where the time goes in v1:
time: 1690 us; the launch traced here: 1670 us
  starting transfers between devices  784 us (46%)
  waiting for transfers between devices  490 us (29%)
  local copies, waits for them, and re-layouts  125 us (7%)
  matrix products  117 us (7%)
  blocking collectives  76.5 us (5%)
  other arithmetic  55.6 us (3%)
    ppermute x72, starting transfers between devices, padded_2(): before = lax.ppermute(last, axis, up)  393 us
    ppermute x69, starting transfers between devices, passed_along(): lax.ppermute(value, axis, [(source, source + steps) for source in range(l...  298 us
    ppermute x69, waiting for transfers between devices, passed_along(): lax.ppermute(value, axis, [(source, source + steps) for source in range(l...  278 us
    psum x2, waiting for transfers between devices, compute_the_side(): w_in = lax.psum(w_in, tick)  136 us
    dot_general x639, matrix products, taps_product(): jnp.dot(window, kernel[row_tap, col_tap], preferred_element_type=jnp.floa...  112 us
    ppermute x72, starting transfers between devices, padded_2(): after = lax.ppermute(leading, axis, down)  93.2 us
    slice x119, local copies, waits for them, and re-layouts, taps_product(): padded[row_tap:row_tap + row_count, col_tap:col_tap + col_count]  79.4 us
    psum x2, blocking collectives, compute_the_side(): w_in = lax.psum(w_in, tick)  76.5 us
  transfers between devices with their start and end apart: 215, of which 133 were waited for; matrix products, arithmetic and copies ran while one was open for 4% of the time, Pallas kernels for 0%

profile of v1, /device:TPU:1, one launch (start us, length us, event | category | flops | bytes accessed | tf_op | source)
XLA Modules:
  0.0 1671.5 jit_solution(5668342432423458111)
XLA Ops:
  128.3 579.6 %while.36 = (s32[]{:T(128)}, f32[2,128,128]{2,1,0:T(8,128)S(1)}, f32[2,128,128]{2,1,0:T(8,128)S(1)}, bf16[3,3,128,128]{3,2,1,0:T(8,128)(2,1)S(1)}, f32[128]{0:T(...) while((s32[]{:T(128)}, f32[2,128,128]{2,1,0:T(8,128)S(1)}, ...), condition=%wide.region_4.5_spmd.clone, body=%wide.region_3.4_spmd.clone.sunk | while | flops 76853248 | bytes 6327017 | solution.py:125
  357.1 7.6 collective-permute-start.2
  376.0 7.6 collective-permute-start.2
  395.0 7.6 collective-permute-start.2
  414.0 7.6 collective-permute-start.2
  432.9 7.6 collective-permute-start.2
  451.9 7.6 collective-permute-start.2
  470.8 7.6 collective-permute-start.2
  489.8 7.6 collective-permute-start.2
  508.8 7.6 collective-permute-start.2
  527.7 7.6 collective-permute-start.2
  546.7 7.6 collective-permute-start.2
  565.7 7.6 collective-permute-start.2
  584.6 7.6 collective-permute-start.2
  603.6 7.6 collective-permute-start.2
  641.5 7.6 collective-permute-start.2
  679.5 7.6 collective-permute-start.2
  810.2 578.3 %while.37 = (s32[]{:T(128)}, f32[2,128,128]{2,1,0:T(8,128)S(1)}, f32[2,128,128]{2,1,0:T(8,128)S(1)}, f32[2,128,128]{2,1,0:T(8,128)S(1)}, bf16[3,3,128,128]{3,2,1...) while((s32[]{:T(128)}, f32[2,128,128]{2,1,0:T(8,128)S(1)}, ...), condition=%wide.region_8.9_spmd.clone, body=%wide.region_7.8_spmd.clone.sunk | while | flops 76886016 | bytes 6457577 | solution.py:147
  821.9 11.0 collective-permute-done.5
  859.8 11.0 collective-permute-done.5
  898.1 11.2 collective-permute-done.5
  1441.8 136.4 %all-reduce.13.cloned.1.call-done = f32[3,3,128,128]{3,2,1,0:T(8,128)} async-done(((f32[3,3,128,128]{3,2,1,0:T(8,128)}), f32[3,3,128,128]{3,2,1,0:T(8,128)}) %all-reduce.13.cloned.1.call-update) | async-done | bytes 589840 | tf_op jit(solution)/shard_map/psum | solution.py:13
  1585.7 62.4 %psum.30 = f32[128]{0:T(128)S(1)} all-reduce(f32[128]{0:T(128)S(1)} %add.603), channel_id=1, replica_groups=mesh['depth'=32,'rows'=8] {'depth'}, use_global_device_ids=true, to_apply=%region_13.14 | all-reduce | flops 128 | bytes 1024 | tf_op jit(solution)/shard_map/psum | solution.py:13
  1648.1 14.1 psum.31
  (1772 shorter events, 1280.1 us)
Async XLA Ops:
  7.2 1571.0 %all-reduce.13.cloned.1.call-start = ((), (), s32[]{:S(2)}) async-start(), calls=%async_computation | async-start | bytes 1179648 | tf_op jit(solution)/shard_map/psum | solution.py:13
  8.4 13.3 collective-permute-start.17
  27.8 16.5 collective-permute-start.11
  31.3 14.2 collective-permute-start.12
  35.0 14.3 collective-permute-start.18
  39.0 10.3 collective-permute-start.19
  40.3 20.0 %collective-permute-start.7 = (bf16[1,256,128]{1,2,0:T(8,128)(2,1)}, bf16[1,256,128]{1,2,0:T(8,128)(2,1)S(1)}, u32[]{:S(2)}, u32[]{:S(2)}) collective-permute-start(bf16[1,256,128]{1,2,0:T(8,128)(2,1)} %get-tuple-element.543), channel_id=1, source_target_pairs={{0,1},{1,2},{2,3},{3,4},{4,5},{5,6},{6,7},{8,9},{9,10},{10,11},{11... | collective-permute-start | bytes 196616 | tf_op jit(solution)/shard_map/ppermute | solution.py:24
  44.3 16.0 collective-permute-start.8
  85.2 13.3 collective-permute-start.10
  86.5 12.0 collective-permute-start.9
  357.1 9.5 collective-permute-start.2
  395.0 9.5 collective-permute-start.2
  432.9 9.5 collective-permute-start.2
  470.8 9.5 collective-permute-start.2
  489.8 9.5 collective-permute-start.2
  709.3 13.0 collective-permute-start.13
  724.2 15.7 collective-permute-start.14
  730.0 9.9 collective-permute-start.15
  732.5 42.3 %collective-permute-start.16 = (f32[2,128,128]{2,1,0:T(8,128)S(1)}, f32[2,128,128]{2,1,0:T(8,128)}, u32[]{:S(2)}, u32[]{:S(2)}) collective-permute-start(f32[2,128,128]{2,1,0:T(8,128)S(1)} %get-tuple-element.361), channel_id=1, source_target_pairs={{0,8},{8,16},{16,24},{24,32},{32,40},{40,48},{48,56},{56,64},{64,7... | collective-permute-start | bytes 393224 | tf_op jit(solution)/shard_map/ppermute | solution.py:33
  819.9 12.9 collective-permute-start.5
  857.8 12.9 collective-permute-start.5
  896.2 13.1 collective-permute-start.5
  1390.8 14.2 collective-permute-start.22
  1441.7 221.0 %all-reduce.15.cloned.1.call-start = ((), (), s32[]{:S(2)}) async-start(), calls=%async_computation.1 | async-start | bytes 1179648 | tf_op jit(solution)/shard_map/psum | solution.py:13
  (275 other events, 3151.9 us)
Sparse Core Ops, SparseCore 0:
  1441.8 136.3 all-reduce.12
  1580.5 69.4 all-reduce.14
